TPU v7x, 512 devices: a whole 4x4x16 slice. The times are simulated.
512 devices in a mesh: gx: 64 (over y, z), gy: 8 (over x, core).
Axes of the slice: x: 4, y: 4, z: 16, core: 2. Of those that a mesh axis runs over, the one named last changes fastest.
Arguments:
- thermal_field: float32 [8, 256, 8192], P(None, 'gy', 'gx'), may hold values from -6 to 6
- material_state: int32 [8, 256, 8192], P(None, 'gy', 'gx'), may hold values from 0 to 2
- beam_path_indicator: int32 [8, 256, 8192], P(None, 'gy', 'gx'), may hold values 0 or 1
- state_diffusivity_table: float32 [3], replicated, may hold values from 0.5 to 2
Outputs:
- new_temperature: float32 [8, 256, 8192], P(None, 'gy', 'gx')
All inputs are finite; a program needn't handle non-finite values. No bound on the sum of `beam_path_indicator` on one device may be relied on, other than what follows from the above.
Results may differ from a plain program's by a relative error of at most 0.02.
Values sent between devices are 32-bit elements; how exact they have to be, the bound alone decides.
A program may use at most 64 MiB of HBM per device.

v0:
```python
import jax
import jax.numpy as jnp
from jax import lax
from jax.sharding import PartitionSpec as P

ratio_x = 65536.0
transverse_step_quotient = 1.0
energy_input_factor = 4.0


def with_halo(value, sides, width):
    for axis, dim in sides:
        devices, length = (lax.axis_size(axis), value.shape[dim])
        up = [(i, (i + 1) % devices) for i in range(devices - 1)]
        down = [(j, i) for i, j in up]
        last = lax.slice_in_dim(value, length - width, length, axis=dim)
        initial = lax.slice_in_dim(value, 0, width, axis=dim)
        before = lax.ppermute(last, axis, up)
        after = lax.ppermute(initial, axis, down)
        value = jnp.concatenate([before, value, after], axis=dim)
    return value


def face_value(first, second):
    return 2.0 * first * second / (first + second)


def summed_spreading(temp_pad, cond_pad, axis):
    count = temp_pad.shape[axis]
    upper_temp = lax.slice_in_dim(temp_pad, 1, count, axis=axis)
    lower_temp = lax.slice_in_dim(temp_pad, 0, count - 1, axis=axis)
    upper_cond = lax.slice_in_dim(cond_pad, 1, count, axis=axis)
    lower_cond = lax.slice_in_dim(cond_pad, 0, count - 1, axis=axis)
    flux = face_value(upper_cond, lower_cond) * (upper_temp - lower_temp)
    return lax.slice_in_dim(flux, 1, count - 1, axis=axis) - lax.slice_in_dim(
        flux, 0, count - 2, axis=axis
    )


def rows_below(values, stride, axis, filler):
    count = values.shape[axis]
    pad_shape = list(values.shape)
    pad_shape[axis] = stride
    padding = jnp.full(pad_shape, filler, values.dtype)
    return jnp.concatenate([padding, lax.slice_in_dim(values, 0, count - stride, axis=axis)], axis)


def rows_above(values, stride, axis, filler):
    count = values.shape[axis]
    pad_shape = list(values.shape)
    pad_shape[axis] = stride
    padding = jnp.full(pad_shape, filler, values.dtype)
    return jnp.concatenate([lax.slice_in_dim(values, stride, count, axis=axis), padding], axis)


def cyclic_solve(lower, diag, upper, sides, axis):
    pencil_count = diag.shape[axis]
    stride = 1
    while stride < pencil_count:
        below_low = rows_below(lower, stride, axis, 0.0)
        below_diag = rows_below(diag, stride, axis, 1.0)
        below_up = rows_below(upper, stride, axis, 0.0)
        above_low = rows_above(lower, stride, axis, 0.0)
        above_diag = rows_above(diag, stride, axis, 1.0)
        above_up = rows_above(upper, stride, axis, 0.0)
        factor_low = lower / below_diag
        factor_up = upper / above_diag
        diag = diag - factor_low * below_up - factor_up * above_low
        lower = -factor_low * below_low
        upper = -factor_up * above_up
        sides = tuple(
            (
                side
                - factor_low * rows_below(side, stride, axis, 0.0)
                - factor_up * rows_above(side, stride, axis, 0.0)
                for side in sides
            )
        )
        stride = stride * 2
    return tuple((side / diag for side in sides))


def solve_block(block):
    return cyclic_solve(block[0], block[1], block[2], (block[3],), 0)[0]


def local(thermal_field, material_state, beam_path_indicator, state_diffusivity_table):
    local_diffusivity_coefficient = jnp.zeros(thermal_field.shape, jnp.float32)
    for material in range(3):
        local_diffusivity_coefficient = local_diffusivity_coefficient + jnp.where(
            material_state == material, state_diffusivity_table[material], 0.0
        )
    padded_thermal_field, padded_diffusivity = (
        with_halo(thermal_field, (("gy", 1),), 1),
        with_halo(local_diffusivity_coefficient, (("gy", 1),), 1),
    )
    spread_second_axis = summed_spreading(padded_thermal_field, padded_diffusivity, 1)
    spacing_third_axis = ((1, 1), (0, 0), (0, 0))
    spread_third_axis = summed_spreading(
        jnp.pad(thermal_field, spacing_third_axis),
        jnp.pad(local_diffusivity_coefficient, spacing_third_axis),
        0,
    )
    known_vector = (
        thermal_field
        + transverse_step_quotient * spread_second_axis
        + transverse_step_quotient * spread_third_axis
        + energy_input_factor * beam_path_indicator.astype(jnp.float32)
    )
    cond_x = with_halo(local_diffusivity_coefficient, (("gx", 2),), 1)
    face_x = face_value(cond_x[:, :, :-1], cond_x[:, :, 1:])
    lower = -ratio_x * face_x[:, :, :-1]
    upper = -ratio_x * face_x[:, :, 1:]
    diag = 1.0 - lower - upper
    pencil_count = thermal_field.shape[2]
    lower = lower.reshape(-1, pencil_count)
    upper = upper.reshape(-1, pencil_count)
    diag = diag.reshape(-1, pencil_count)
    known_vector = known_vector.reshape(-1, pencil_count)
    column = lax.broadcasted_iota(jnp.int32, lower.shape, 1)
    edges = (column == 0) | (column == pencil_count - 1)
    inner_low = jnp.where(edges | (column == 1), 0.0, lower)
    inner_up = jnp.where(edges | (column == pencil_count - 2), 0.0, upper)
    inner_diag = jnp.where(edges, 1.0, diag)
    side_main = jnp.where(edges, 0.0, known_vector)
    side_first = jnp.where(column == 1, -lower, 0.0)
    side_last = jnp.where(column == pencil_count - 2, -upper, 0.0)
    starting_field, leading_coupling, trailing_coupling = cyclic_solve(
        inner_low, inner_diag, inner_up, (side_main, side_first, side_last), 1
    )
    first_low = lower[:, 0]
    first_diag = diag[:, 0] + upper[:, 0] * leading_coupling[:, 1]
    first_up = upper[:, 0] * trailing_coupling[:, 1]
    first_side = known_vector[:, 0] - upper[:, 0] * starting_field[:, 1]
    last_low = lower[:, -1] * leading_coupling[:, -2]
    last_diag = diag[:, -1] + lower[:, -1] * trailing_coupling[:, -2]
    last_up = upper[:, -1]
    last_side = known_vector[:, -1] - lower[:, -1] * starting_field[:, -2]
    coeffs = jnp.stack(
        [
            jnp.stack([first_low, last_low], 0),
            jnp.stack([first_diag, last_diag], 0),
            jnp.stack([first_up, last_up], 0),
            jnp.stack([first_side, last_side], 0),
        ],
        0,
    )
    gathered = lax.all_gather(coeffs, "gx", axis=1, tiled=True)
    answered_pencils = solve_block(gathered)
    own_ends = lax.dynamic_slice_in_dim(answered_pencils, 2 * lax.axis_index("gx"), 2, 0)
    leading_entry = own_ends[0][:, None]
    trailing_entry = own_ends[1][:, None]
    advanced_thermal_field = (
        starting_field + leading_coupling * leading_entry + trailing_coupling * trailing_entry
    )
    advanced_thermal_field = (
        advanced_thermal_field
        + jnp.where(column == 0, leading_entry, 0.0)
        + jnp.where(column == pencil_count - 1, trailing_entry, 0.0)
    )
    return advanced_thermal_field.reshape(thermal_field.shape)


def solution(mesh):
    in_specs = (P(None, "gy", "gx"), P(None, "gy", "gx"), P(None, "gy", "gx"), P())
    out_specs = P(None, "gy", "gx")
    return jax.shard_map(local, mesh=mesh, in_specs=in_specs, out_specs=out_specs, check_vma=False)
```

profile of v0, /device:TPU:6, one launch (start us, length us, event | category | flops | bytes accessed | tf_op | source)
XLA Modules:
  0.0 137.6 jit_solution(11413392106843344110)
XLA Ops:
  0.0 1.4 %fusion.104 = (f32[1]{0:T(128)}, f32[1]{0:T(128)}, f32[1]{0:T(128)}) fusion(f32[3]{0:T(128)} %param.7), kind=kLoop, calls=%fused_computation.252 | loop fusion | bytes 24 | tf_op jit(solution)/shard_map/slice | solution.py:91
  1.4 2.9 %select_add_fusion.1 = f32[8,32,128]{2,1,0:T(8,128)S(1)} fusion(s32[8,32,128]{2,1,0:T(8,128)} %param.5, f32[]{:T(128)} %bitcast.2, f32[]{:T(128)} %bitcast.1, f32[]{:T(128)} %bitcast), kind=kLoop, calls=%fused_computation.128 | loop fusion | flops 262144 | bytes 262156 | tf_op jit(solution)/shard_map/add | solution.py:90
  4.3 2.2 %collective-permute-start = (f32[8,1,128]{2,1,0:T(1,128)S(1)}, f32[8,1,128]{2,1,0:T(1,128)S(1)}, u32[]{:S(2)}, u32[]{:S(2)}) collective-permute-start(f32[8,1,128]{2,1,0:T(1,128)S(1)} %get-tuple-element.180), channel_id=1, source_target_pairs={{1,0},{2,1},{3,2},{4,3},{5,4},{6,5},{7,6},{9,8},{10,9},{11,10},{12... | collective-permute-start | bytes 12296 | tf_op jit(solution)/shard_map/ppermute | solution.py:19
  6.5 2.1 %collective-permute-start.1 = (f32[8,1,128]{2,1,0:T(1,128)S(1)}, f32[8,1,128]{2,1,0:T(1,128)S(1)}, u32[]{:S(2)}, u32[]{:S(2)}) collective-permute-start(f32[8,1,128]{2,1,0:T(1,128)S(1)} %get-tuple-element.181), channel_id=1, source_target_pairs={{0,1},{1,2},{2,3},{3,4},{4,5},{5,6},{6,7},{8,9},{9,10},{10,11},{11... | collective-permute-start | bytes 12296 | tf_op jit(solution)/shard_map/ppermute | solution.py:18
  8.7 3.4 %collective-permute-start.2 = (f32[8,1,128]{2,1,0:T(1,128)S(1)}, f32[8,1,128]{2,1,0:T(1,128)S(1)}, u32[]{:S(2)}, u32[]{:S(2)}) collective-permute-start(f32[8,1,128]{2,1,0:T(1,128)S(1)} %get-tuple-element.183), channel_id=1, source_target_pairs={{1,0},{2,1},{3,2},{4,3},{5,4},{6,5},{7,6},{9,8},{10,9},{11,10},{12... | collective-permute-start | bytes 12296 | tf_op jit(solution)/shard_map/ppermute | solution.py:19
  12.2 3.8 %collective-permute-start.4 = (f32[8,32,1]{2,1,0:T(8,128)S(1)}, f32[8,32,1]{2,1,0:T(8,128)S(1)}, u32[]{:S(2)}, u32[]{:S(2)}) collective-permute-start(f32[8,32,1]{2,1,0:T(8,128)S(1)} %get-tuple-element.249), channel_id=1, source_target_pairs={{0,8},{8,16},{16,24},{24,32},{32,40},{40,48},{48,56},{56,64},{64,7... | collective-permute-start | bytes 3080 | tf_op jit(solution)/shard_map/ppermute | solution.py:18
  16.1 1.3 collective-permute-start.5
  17.5 1.1 collective-permute-done.4
  18.6 1.9 %collective-permute-start.3 = (f32[8,1,128]{2,1,0:T(1,128)S(1)}, f32[8,1,128]{2,1,0:T(1,128)S(1)}, u32[]{:S(2)}, u32[]{:S(2)}) collective-permute-start(f32[8,1,128]{2,1,0:T(1,128)S(1)} %get-tuple-element.182), channel_id=1, source_target_pairs={{0,1},{1,2},{2,3},{3,4},{4,5},{5,6},{6,7},{8,9},{9,10},{10,11},{11... | collective-permute-start | bytes 12296 | tf_op jit(solution)/shard_map/ppermute | solution.py:18
  20.5 2.4 %collective-permute-done.5 = f32[8,32,1]{2,1,0:T(8,128)S(1)} collective-permute-done((f32[8,32,1]{2,1,0:T(8,128)S(1)}, f32[8,32,1]{2,1,0:T(8,128)S(1)}, u32[]{:S(2)}, u32[]{:S(2)}) %collective-permute-start.5) | collective-permute-done | bytes 1056 | tf_op jit(solution)/shard_map/ppermute | solution.py:19
  22.9 0.1 add_divide_fusion
  23.1 0.1 slice_multiply_fusion
  23.2 0.1 copy.21
  23.5 0.1 copy.23
  23.7 0.8 copy-done.1
  24.8 0.1 multiply_subtract_fusion.21
  25.2 0.2 multiply_subtract_fusion.34
  25.5 0.2 multiply_subtract_fusion.32
  25.9 0.2 multiply_subtract_fusion.30
  26.3 0.2 multiply_subtract_fusion.28
  26.6 0.1 multiply_subtract_fusion.26
  26.9 0.1 multiply_subtract_fusion.24
  27.4 106.6 %all_gather.3 = f32[4,128,256]{2,0,1:T(4,128)S(1)} all-gather(f32[4,2,256]{2,0,1:T(4,128)S(1)} %copy.34), channel_id=1, replica_groups=mesh['gx'=64,'gy'=8] {'gx'}, dimensions={1}, use_global_device_ids=true | all-gather | bytes 532480 | tf_op jit(solution)/shard_map/all_gather | solution.py:148
  133.9 0.6 fusion.36
  134.5 0.4 fusion.37
  135.2 0.1 multiply_subtract_fusion.9
  135.5 0.1 multiply_subtract_fusion.7
  135.8 0.1 multiply_subtract_fusion.5
  136.1 0.1 multiply_subtract_fusion.3
  136.4 0.1 multiply_subtract_fusion.1
  136.7 0.1 select_add_fusion
  136.9 0.8 copy.46
  (118 shorter events, 2.8 us)
Async XLA Ops:
  1.4 7.3 %copy-start = (f32[8,32,128]{2,1,0:T(8,128)S(1)}, f32[8,32,128]{2,1,0:T(8,128)}, u32[]{:S(2)}) copy-start(f32[8,32,128]{2,1,0:T(8,128)} %param.4) | copy-start | bytes 393220
  4.3 19.3 %collective-permute-start = (f32[8,1,128]{2,1,0:T(1,128)S(1)}, f32[8,1,128]{2,1,0:T(1,128)S(1)}, u32[]{:S(2)}, u32[]{:S(2)}) collective-permute-start(f32[8,1,128]{2,1,0:T(1,128)S(1)} %get-tuple-element.180), channel_id=1, source_target_pairs={{1,0},{2,1},{3,2},{4,3},{5,4},{6,5},{7,6},{9,8},{10,9},{11,10},{12... | collective-permute-start | bytes 12296 | tf_op jit(solution)/shard_map/ppermute | solution.py:19
  6.5 17.1 %collective-permute-start.1 = (f32[8,1,128]{2,1,0:T(1,128)S(1)}, f32[8,1,128]{2,1,0:T(1,128)S(1)}, u32[]{:S(2)}, u32[]{:S(2)}) collective-permute-start(f32[8,1,128]{2,1,0:T(1,128)S(1)} %get-tuple-element.181), channel_id=1, source_target_pairs={{0,1},{1,2},{2,3},{3,4},{4,5},{5,6},{6,7},{8,9},{9,10},{10,11},{11... | collective-permute-start | bytes 12296 | tf_op jit(solution)/shard_map/ppermute | solution.py:18
  8.7 14.9 %collective-permute-start.2 = (f32[8,1,128]{2,1,0:T(1,128)S(1)}, f32[8,1,128]{2,1,0:T(1,128)S(1)}, u32[]{:S(2)}, u32[]{:S(2)}) collective-permute-start(f32[8,1,128]{2,1,0:T(1,128)S(1)} %get-tuple-element.183), channel_id=1, source_target_pairs={{1,0},{2,1},{3,2},{4,3},{5,4},{6,5},{7,6},{9,8},{10,9},{11,10},{12... | collective-permute-start | bytes 12296 | tf_op jit(solution)/shard_map/ppermute | solution.py:19
  12.2 6.3 %collective-permute-start.4 = (f32[8,32,1]{2,1,0:T(8,128)S(1)}, f32[8,32,1]{2,1,0:T(8,128)S(1)}, u32[]{:S(2)}, u32[]{:S(2)}) collective-permute-start(f32[8,32,1]{2,1,0:T(8,128)S(1)} %get-tuple-element.249), channel_id=1, source_target_pairs={{0,8},{8,16},{16,24},{24,32},{32,40},{40,48},{48,56},{56,64},{64,7... | collective-permute-start | bytes 3080 | tf_op jit(solution)/shard_map/ppermute | solution.py:18
  16.1 6.9 %collective-permute-start.5 = (f32[8,32,1]{2,1,0:T(8,128)S(1)}, f32[8,32,1]{2,1,0:T(8,128)S(1)}, u32[]{:S(2)}, u32[]{:S(2)}) collective-permute-start(f32[8,32,1]{2,1,0:T(8,128)S(1)} %get-tuple-element.250), channel_id=1, source_target_pairs={{8,0},{16,8},{24,16},{32,24},{40,32},{48,40},{56,48},{64,56},{72,6... | collective-permute-start | bytes 3080 | tf_op jit(solution)/shard_map/ppermute | solution.py:19
  18.6 5.1 %collective-permute-start.3 = (f32[8,1,128]{2,1,0:T(1,128)S(1)}, f32[8,1,128]{2,1,0:T(1,128)S(1)}, u32[]{:S(2)}, u32[]{:S(2)}) collective-permute-start(f32[8,1,128]{2,1,0:T(1,128)S(1)} %get-tuple-element.182), channel_id=1, source_target_pairs={{0,1},{1,2},{2,3},{3,4},{4,5},{5,6},{6,7},{8,9},{9,10},{10,11},{11... | collective-permute-start | bytes 12296 | tf_op jit(solution)/shard_map/ppermute | solution.py:18
  23.6 0.9 copy-start.1
where the time goes:
time: 138 us
  blocking collectives  107 us (78%)
  starting transfers between devices  14.8 us (11%)
  other arithmetic  6.13 us (4%)
  local copies, waits for them, and re-layouts  5.57 us (4%)
  waiting for transfers between devices  3.54 us (3%)
    all_gather x1, blocking collectives, local(): gathered = lax.all_gather(coeffs, 'gx', axis=1, tiled=True)  107 us
    ppermute x3, starting transfers between devices, with_halo(): before = lax.ppermute(last, axis, up)  7.88 us
    ppermute x3, starting transfers between devices, with_halo(): after = lax.ppermute(initial, axis, down)  6.88 us
    add x1, other arithmetic, local(): local_diffusivity_coefficient + jnp.where(material_state == material, sta...  2.89 us
  transfers between devices with their start and end apart: 6, of which 2 were waited for; matrix products, arithmetic and copies ran while one was open for 1% of the time, Pallas kernels for 0%

commit v1 on v0

v1 whole, which is shorter than its diff:
```python
import jax
import jax.numpy as jnp
from jax import lax
from jax.experimental import pallas as pl
from jax.experimental.pallas import tpu as pltpu
from jax.sharding import PartitionSpec as P

MESH = pl.DeviceIdType.MESH
RATIO = 65536.0
NSEG = 64
NGY = 8
NEAR = (-3, -2, -1, 1, 2, 3, 4)
FAR = (4, 12, 20, 28, 36, 44, 52, 60)


def face(a, b):
    return 2.0 * a * b / (a + b)


def split(x):
    high = 4097.0 * x
    high = high - (high - x)
    return high, x - high


def exact_face(a, b):
    above, below = 2.0 * a * b, a + b
    q = above / below
    (qh, ql), (bh, bl) = split(q), split(below)
    p = q * below
    error = ((qh * bh - p) + qh * bl + ql * bh) + ql * bl
    return q + ((above - p) - error) / below


def shunt_of(left, right):
    once = 1.0 + left
    diag = once + right
    part = diag - once
    return (once - left) - ((once - (diag - part)) + (right - part))


def combine(a, b):
    ab, aal, abe, as1, as2 = a
    bb, bal, bbe, bs1, bs2 = b
    shunt = abe + bal
    r = 1.0 / (ab + bb + shunt)
    pa, pb = ab * r, bb * r
    s = as2 + bs1
    return (pa * bb, aal + pa * shunt, bbe + pb * shunt, as1 + pa * s, bs2 + pb * s)


def build(g, shunts, lo, hi):
    if hi - lo == 1:
        return (g[lo], shunts[lo], None), []
    half = 1
    while half * 2 < hi - lo:
        half *= 2
    mid = lo + half
    (ab, aal, abe), left = build(g, shunts, lo, mid)
    (bb, bal, bbe), right = build(g, shunts, mid, hi)
    shunt = bal if abe is None else bal + abe
    r = 1.0 / (ab + bb + shunt)
    pa, pb = ab * r, bb * r
    al = aal + pa * shunt
    be = pb * shunt if bbe is None else bbe + pb * shunt
    return (pa * bb, al, be), left + right + [(mid, lo, hi, pa, pb, r)]


def kernel(
    t_hbm, m_hbm, b_hbm, table, out_ref,
    tv, mv, bv, cv, fv, trans, pq, edge, elim, hs, hr, xs, xr, own, mine, near, mid, far,
    load_sem, hs_sem, hr_sem, xs_sem, xr_sem, ns_sem, nr_sem, fs_sem, fr_sem,
):
    gx, gy = lax.axis_index("gx"), lax.axis_index("gy")

    loads = [
        pltpu.make_async_copy(src, dst, load_sem.at[k])
        for k, (src, dst) in enumerate(((m_hbm, mv), (t_hbm, tv), (b_hbm, bv)))
    ]
    for load in loads:
        load.start()

    def seg(offset):
        return {"gx": lax.rem(gx + (offset % NSEG), NSEG)}

    def side(offset):
        return {"gy": lax.rem(gy + (offset % NGY), NGY)}

    barrier = pltpu.get_barrier_semaphore()
    senders = [seg(o) for o in sorted(set(o % NSEG for o in NEAR + FAR))] + [side(1), side(-1)]
    for device in senders:
        pl.semaphore_signal(barrier, inc=1, device_id=device, device_id_type=MESH)

    loads[0].wait()
    t0, t1, t2 = table[0], table[1], table[2]
    m = mv[...]
    cv[...] = jnp.where(m == 0, t0, jnp.where(m == 1, t1, t2))
    loads[1].wait()
    hs[0, 0] = tv[pl.ds(0, 8, stride=32), :]
    hs[0, 1] = cv[pl.ds(0, 8, stride=32), :]
    hs[1, 0] = tv[pl.ds(31, 8, stride=32), :]
    hs[1, 1] = cv[pl.ds(31, 8, stride=32), :]
    for h in range(2):
        trans[h] = cv[128 * h : 128 * h + 128, :].T
        xs[0, h : h + 1, :] = trans[h, 0:1, :]
        xs[1, h : h + 1, :] = trans[h, 127:128, :]

    pl.semaphore_wait(barrier, len(senders))
    halo = [
        pltpu.make_async_remote_copy(
            src_ref=hs.at[k], dst_ref=hr.at[1 - k], send_sem=hs_sem.at[k], recv_sem=hr_sem.at[1 - k],
            device_id=side(2 * k - 1), device_id_type=MESH,
        )
        for k in range(2)
    ]
    halo_x = [
        pltpu.make_async_remote_copy(
            src_ref=xs.at[k], dst_ref=xr.at[1 - k], send_sem=xs_sem.at[k], recv_sem=xr_sem.at[1 - k],
            device_id=seg(2 * k - 1), device_id_type=MESH,
        )
        for k in range(2)
    ]
    for copy in halo + halo_x:
        copy.start()

    shape = (2, 8, 128)
    row = lax.broadcasted_iota(jnp.int32, shape, 1)

    tables = [jnp.full((8, 128), t, jnp.float32) for t in (t0, t1, t2)]
    faces = {}
    for i in range(3):
        for j in range(i, 3):
            faces[i, j] = faces[j, i] = RATIO * exact_face(tables[i], tables[j])[0:1, :]

    def joint(a, b):
        b0, b1 = b == t0, b == t1
        rows = [jnp.where(b0, faces[i, 0], jnp.where(b1, faces[i, 1], faces[i, 2])) for i in range(3)]
        return jnp.where(a == t0, rows[0], jnp.where(a == t1, rows[1], rows[2]))

    def piece(j):
        return jnp.stack([trans[h, pl.ds(j, 8, stride=16), :] for h in range(2)])

    cond = [piece(j) for j in range(16)]
    cond.append(pltpu.roll(cond[0], 7, 1))
    g = [joint(cond[j], cond[j + 1]) for j in range(16)]
    last = row == 7
    shunts = [jnp.where(row == 0, 0.0, shunt_of(pltpu.roll(g[15], 1, 1), g[0]))]
    shunts += [shunt_of(g[j - 1], g[j]) for j in range(1, 16)]
    (cb, cal, cbe), steps = build(g, shunts, 0, 15)
    cbe = cbe + jnp.where(last, 0.0, shunts[15])
    r15 = 1.0 / (cb + cbe + g[15])
    pa15, pb15 = cb * r15, g[15] * r15
    b = jnp.where(last, cb, pa15 * g[15])
    al = jnp.where(last, cal, cal + pa15 * cbe)
    be = jnp.where(last, cbe, pb15 * cbe)
    levels = []
    for step in (1, 2, 4):
        bb, bal, bbe = (pltpu.roll(v, 8 - step, 1) for v in (b, al, be))
        shunt = be + bal
        r = 1.0 / (b + bb + shunt)
        pa, pb = b * r, bb * r
        b, al, be = pa * bb, al + pa * shunt, bbe + pb * shunt
        levels.append((step, pa, pb, r))
    for h in range(2):
        own[0, h : h + 1, :] = b[h, 0:1, :]
        own[1, h : h + 1, :] = al[h, 0:1, :]
        own[2, h : h + 1, :] = be[h, 0:1, :]
        own[5, h : h + 1, :] = g[0][h, 0:1, :]
        own[6, h : h + 1, :] = g[14][h, 7:8, :]

    def spread(value, step):
        if step == 4:
            return jnp.broadcast_to(value[:, 0:1, :], shape)
        if step == 2:
            return jnp.where(row < 4, value[:, 0:1, :], value[:, 4:5, :])
        return jnp.where(row % 2 == 0, value, pltpu.roll(value, 1, 1))

    def descend(left, right, sources):
        for k, (step, pa, pb, _) in reversed(list(enumerate(levels))):
            centre = pa * left + pb * right
            if sources is not None:
                centre = centre + sources[0][k]
            centre = spread(centre, step)
            low = (row // step) % 2 == 0
            left, right = jnp.where(low, left, centre), jnp.where(low, centre, right)
        end = pa15 * left + pb15 * right
        if sources is not None:
            end = end + sources[1]
        values = {0: left, 15: jnp.where(last, right, end)}
        for node, lo, hi, pa, pb, _ in reversed(steps):
            values[node] = pa * values[lo] + pb * values[hi]
            if sources is not None:
                values[node] = values[node] + sources[2][node]
        return [values[j] for j in range(16)]

    one, zero = jnp.ones(shape, jnp.float32), jnp.zeros(shape, jnp.float32)
    for j, value in enumerate(descend(one, zero, None)):
        pq[0, j] = value
    for j, value in enumerate(descend(zero, one, None)):
        pq[1, j] = value
    for k, (_, _, _, _, _, r) in enumerate(steps):
        elim[k] = r

    loads[2].wait()
    line = lax.broadcasted_iota(jnp.int32, (32, 128), 0)
    below = None
    for z in range(8):
        here = slice(32 * z, 32 * z + 32)
        tz, cz = tv[here, :], cv[here, :]
        flux = jnp.where(line < 31, face(cz, pltpu.roll(cz, 31, 0)) * (pltpu.roll(tz, 31, 0) - tz), 0.0)
        value = tz + (flux - pltpu.roll(flux, 1, 0)) + 4.0 * bv[here, :].astype(jnp.float32)
        if below is not None:
            value = value - below
        if z < 7:
            above = slice(32 * z + 32, 32 * z + 64)
            below = face(cz, cv[above, :]) * (tv[above, :] - tz)
            value = value + below
        fv[here, :] = value

    for copy in halo:
        copy.wait_recv()
    low, high = pl.ds(0, 8, stride=32), pl.ds(31, 8, stride=32)
    flux = face(hs[1, 1], hr[1, 1]) * (hr[1, 0] - hs[1, 0])
    fv[high, :] = fv[high, :] + jnp.where(gy < NGY - 1, flux, 0.0)
    flux = face(hs[0, 1], hr[0, 1]) * (hs[0, 0] - hr[0, 0])
    fv[low, :] = fv[low, :] - jnp.where(gy > 0, flux, 0.0)
    for h in range(2):
        trans[h] = fv[128 * h : 128 * h + 128, :].T

    first, second = zero, zero
    for j in range(16):
        f = piece(j)
        first, second = first + pq[0, j] * f, second + pq[1, j] * f
    for h in range(2):
        own[3, h : h + 1, :] = jnp.sum(first[h], axis=0, keepdims=True)
        own[4, h : h + 1, :] = jnp.sum(second[h], axis=0, keepdims=True)

    for copy in halo_x:
        copy.wait_recv()
    ob, oal, obe, os1, os2, first_g, last_g = (own[k] for k in range(7))
    og = jnp.where(gx < NSEG - 1, joint(xs[1], xr[1]), 0.0)
    oal = oal + shunt_of(jnp.where(gx > 0, joint(xr[0], xs[0]), 0.0), first_g)
    obe = obe + shunt_of(last_g, og)
    r = 1.0 / (ob + obe + og)
    pa, pb = ob * r, og * r
    whole = (pa * og, oal + pa * obe, pb * obe, os1 + pa * os2, pb * os2)
    for k in range(5):
        mine[k] = whole[k]
    near_copies = [
        pltpu.make_async_remote_copy(
            src_ref=mine, dst_ref=near.at[k], send_sem=ns_sem.at[k], recv_sem=nr_sem.at[k],
            device_id=seg(-o), device_id_type=MESH,
        )
        for k, o in enumerate(NEAR)
    ]
    for k in (6, 5, 0, 4, 1, 3, 2):
        near_copies[k].start()

    steps = [(node, lo, hi, pa, pb, elim[k]) for k, (node, lo, hi, pa, pb, _) in enumerate(steps)]
    f = [piece(j) for j in range(16)]
    ends = {(j, j + 1): (f[j], None) for j in range(15)}
    inner = {}
    for node, lo, hi, pa, pb, r in steps:
        a, c = ends[lo, node], ends[node, hi]
        s = c[0] if a[1] is None else a[1] + c[0]
        inner[node] = s * r
        ends[lo, hi] = (a[0] + pa * s, pb * s if c[1] is None else c[1] + pb * s)
    s1, s2 = ends[0, 15]
    s2 = s2 + f[15]
    at_end = r15 * s2
    s1, s2 = jnp.where(last, s1, s1 + pa15 * s2), jnp.where(last, s2, pb15 * s2)
    middle = []
    for step, pa, pb, r in levels:
        bs1, bs2 = pltpu.roll(s1, 8 - step, 1), pltpu.roll(s2, 8 - step, 1)
        s = s2 + bs1
        middle.append(s * r)
        s1, s2 = s1 + pa * s, bs2 + pb * s
    for j, value in enumerate(descend(zero, zero, (middle, at_end, inner))):
        pq[2, j] = value

    for copy in near_copies:
        copy.wait_recv()
    item = {o: tuple(near[k, i] for i in range(5)) for k, o in enumerate(NEAR)}
    item[0] = whole
    ahead = combine(combine(item[1], item[2]), combine(item[3], item[4]))
    behind = combine(item[-3], item[-2])
    behind_own = combine(behind, combine(item[-1], item[0]))
    behind = combine(behind, item[-1])
    window = combine(behind_own, ahead)
    for k in range(5):
        mid[0, k] = ahead[k]
        mid[1, k] = window[k]
        mid[2, k] = behind_own[k]
    far_copies = [
        pltpu.make_async_remote_copy(
            src_ref=mid.at[0 if k == 0 else 2 if k == 7 else 1], dst_ref=far.at[k],
            send_sem=fs_sem.at[k], recv_sem=fr_sem.at[k],
            device_id=seg(-o), device_id_type=MESH,
        )
        for k, o in enumerate(FAR)
    ]
    for k in (3, 4, 2, 5, 1, 6, 0, 7):
        far_copies[k].start()
    for copy in far_copies:
        copy.wait_recv()
    chain = [ahead] + [tuple(far[k, i] for i in range(5)) for k in range(8)] + [behind]
    while len(chain) > 1:
        chain = [combine(*chain[k : k + 2]) if k + 1 < len(chain) else chain[k] for k in range(0, len(chain), 2)]
    _, right_g, left_g, right_s, left_s = chain[0]

    r = og / (og + right_g)
    end_g, end_s = obe + r * right_g, os2 + r * right_s
    r = 1.0 / (ob + end_g)
    start = (os1 + left_s + ob * r * end_s) / (oal + left_g + ob * r * end_g)
    end = r * (ob * start + end_s)
    start = jnp.stack([jnp.broadcast_to(start[h : h + 1, :], (8, 128)) for h in range(2)])
    end = jnp.stack([jnp.broadcast_to(end[h : h + 1, :], (8, 128)) for h in range(2)])
    for j in range(16):
        value = pq[2, j] + pq[0, j] * start + pq[1, j] * end
        for h in range(2):
            trans[h, pl.ds(j, 8, stride=16), :] = value[h]
    for h in range(2):
        out_ref[128 * h : 128 * h + 128, :] = trans[h].T

    for copy in halo + halo_x + near_copies + far_copies:
        copy.wait_send()


def local(thermal_field, material_state, beam_path_indicator, state_diffusivity_table):
    f32 = jnp.float32
    flat = (256, 128)
    hbm = pl.BlockSpec(memory_space=pltpu.HBM)
    dma = pltpu.SemaphoreType.DMA
    out = pl.pallas_call(
        kernel,
        out_shape=jax.ShapeDtypeStruct(flat, f32),
        in_specs=[hbm, hbm, hbm, pl.BlockSpec(memory_space=pltpu.SMEM)],
        out_specs=pl.BlockSpec(memory_space=pltpu.VMEM),
        scratch_shapes=[
            pltpu.VMEM(flat, f32),
            pltpu.VMEM(flat, jnp.int32),
            pltpu.VMEM(flat, jnp.int32),
            pltpu.VMEM(flat, f32),
            pltpu.VMEM(flat, f32),
            pltpu.VMEM((2, 128, 128), f32),
            pltpu.VMEM((3, 16, 2, 8, 128), f32),
            pltpu.VMEM((8, 128), f32),
            pltpu.VMEM((14, 2, 8, 128), f32),
            pltpu.VMEM((2, 2, 8, 128), f32),
            pltpu.VMEM((2, 2, 8, 128), f32),
            pltpu.VMEM((2, 2, 128), f32),
            pltpu.VMEM((2, 2, 128), f32),
            pltpu.VMEM((7, 2, 128), f32),
            pltpu.VMEM((5, 2, 128), f32),
            pltpu.VMEM((len(NEAR), 5, 2, 128), f32),
            pltpu.VMEM((3, 5, 2, 128), f32),
            pltpu.VMEM((len(FAR), 5, 2, 128), f32),
            dma((3,)),
            dma((2,)),
            dma((2,)),
            dma((2,)),
            dma((2,)),
            dma((len(NEAR),)),
            dma((len(NEAR),)),
            dma((len(FAR),)),
            dma((len(FAR),)),
        ],
        compiler_params=pltpu.CompilerParams(collective_id=0, has_side_effects=True),
        name="adi_x",
    )(
        thermal_field.reshape(flat),
        material_state.reshape(flat),
        beam_path_indicator.reshape(flat),
        state_diffusivity_table,
    )
    return out.reshape(thermal_field.shape)


def solution(mesh):
    in_specs = (P(None, "gy", "gx"), P(None, "gy", "gx"), P(None, "gy", "gx"), P())
    out_specs = P(None, "gy", "gx")
    return jax.shard_map(local, mesh=mesh, in_specs=in_specs, out_specs=out_specs, check_vma=False)
```

time: 138 us -> 33.9 us (0.25)
  blocking collectives: 107 us -> 0 us
  Pallas kernels: 0 us -> 32.1 us
  starting transfers between devices: 14.8 us -> 0 us
  other arithmetic: 6.13 us -> 0 us
  local copies, waits for them, and re-layouts: 5.57 us -> 1.57 us
  waiting for transfers between devices: 3.54 us -> 0 us
    all_gather x1 -> x0, blocking collectives: 107 us -> none  [local(): gathered = lax.all_gather(coeffs, 'gx', axis=1, tiled=True)]
    pallas_call x0 -> x1, Pallas kernels: none -> 32.1 us  [local(): pl.pallas_call(kernel, out_shape=jax.ShapeDtypeStruct(flat, f32), in_spec...]
    ppermute x6 -> x0, starting transfers between devices: 14.8 us -> none  [the longest x3 7.88 us: with_halo(): before = lax.ppermute(last, axis, up)]
    slice x73 -> x0, local copies, waits for them, and re-layouts: 3.56 us -> none  [the longest x1 1.42 us: local(): state_diffusivity_table[material]]
    ppermute x6 -> x0, waiting for transfers between devices: 3.54 us -> none  [the longest x3 2.45 us: with_halo(): after = lax.ppermute(initial, axis, down)]
    add x3 -> x0, other arithmetic: 3.05 us -> none  [the longest x1 2.89 us: local(): local_diffusivity_coefficient + jnp.where(material_state == material, sta...]
    sub x23 -> x0, other arithmetic: 2.21 us -> none  [the longest x12 1.6 us: cyclic_solve(): side - factor_low * rows_below(side, stride, axis, 0.0)]
  transfers between devices with their start and end apart: 6 -> 0, of which waited for: 2 -> 0; matrix products, arithmetic and copies ran while one was open for 1% -> 0% of each run, Pallas kernels for 0% -> 0%
where the time goes in v1:
time: 33.9 us; the launch traced here: 33.6 us
  Pallas kernels  32.1 us (95%)
  local copies, waits for them, and re-layouts  1.57 us (5%)
    pallas_call x1, Pallas kernels, local(): pl.pallas_call(kernel, out_shape=jax.ShapeDtypeStruct(flat, f32), in_spec...  32.1 us
    unnamed x1, local copies, waits for them, and re-layouts  1.57 us

profile of v1, /device:TPU:6, one launch (start us, length us, event | category | flops | bytes accessed | tf_op | source)
XLA Modules:
  0.0 33.6 jit_solution(11576891534255347773)
XLA Ops:
  0.0 32.1 %adi_x.1 = f32[256,128]{1,0:T(8,128)} custom-call(f32[256,128]{1,0:T(8,128)} %bitcast.5, s32[256,128]{1,0:T(8,128)} %bitcast.6, s32[256,128]{1,0:T(8,128)} %bitcast.7, f32[3]{0:T(128)} %table.1), custom_call_target="tpu_custom_call" | custom-call | tf_op jit(solution)/shard_map/adi_x/pallas_call | solution.py:334
  32.1 1.6 %copy.6 = f32[8,32,128]{2,1,0:T(8,128)} copy(f32[8,32,128]{2,1,0:T(8,128)} %bitcast.4) | data formatting | bytes 262144

commit v2 on v1

--- a/solution.py
+++ b/solution.py
@@ -10,6 +10,7 @@
 NSEG = 64
 NGY = 8
 NEAR = (-3, -2, -1, 1, 2, 3, 4)
+GREET = (-2, -1, 1, 2, 16, 32, 48)
 FAR = (4, 12, 20, 28, 36, 44, 52, 60)
 
 
@@ -68,8 +69,8 @@
 
 def kernel(
     t_hbm, m_hbm, b_hbm, table, out_ref,
-    tv, mv, bv, cv, fv, trans, pq, edge, elim, hs, hr, xs, xr, own, mine, near, mid, far,
-    load_sem, hs_sem, hr_sem, xs_sem, xr_sem, ns_sem, nr_sem, fs_sem, fr_sem,
+    tv, mv, bv, cv, fv, trans, pq, elim, hs, hr, xs, xr, own, mine, near, mid, far,
+    load_sem, hs_sem, hr_sem, xs_sem, xr_sem, ns_sem, nr_sem, fs_sem, fr_sem, word_sem,
 ):
     gx, gy = lax.axis_index("gx"), lax.axis_index("gy")
 
@@ -87,25 +88,24 @@
         return {"gy": lax.rem(gy + (offset % NGY), NGY)}
 
     barrier = pltpu.get_barrier_semaphore()
-    senders = [seg(o) for o in sorted(set(o % NSEG for o in NEAR + FAR))] + [side(1), side(-1)]
-    for device in senders:
+    greeted = [side(1), side(-1)] + [seg(o) for o in GREET]
+    for device in greeted:
         pl.semaphore_signal(barrier, inc=1, device_id=device, device_id_type=MESH)
 
+    t0, t1, t2 = table[0], table[1], table[2]
+
+    def conductivity(m):
+        return jnp.where(m == 0, t0, jnp.where(m == 1, t1, t2))
+
+    low, high = pl.ds(0, 8, stride=32), pl.ds(31, 8, stride=32)
     loads[0].wait()
-    t0, t1, t2 = table[0], table[1], table[2]
-    m = mv[...]
-    cv[...] = jnp.where(m == 0, t0, jnp.where(m == 1, t1, t2))
+    hs[0, 1] = conductivity(mv[low, :])
+    hs[1, 1] = conductivity(mv[high, :])
     loads[1].wait()
-    hs[0, 0] = tv[pl.ds(0, 8, stride=32), :]
-    hs[0, 1] = cv[pl.ds(0, 8, stride=32), :]
-    hs[1, 0] = tv[pl.ds(31, 8, stride=32), :]
-    hs[1, 1] = cv[pl.ds(31, 8, stride=32), :]
-    for h in range(2):
-        trans[h] = cv[128 * h : 128 * h + 128, :].T
-        xs[0, h : h + 1, :] = trans[h, 0:1, :]
-        xs[1, h : h + 1, :] = trans[h, 127:128, :]
-
-    pl.semaphore_wait(barrier, len(senders))
+    hs[0, 0] = tv[low, :]
+    hs[1, 0] = tv[high, :]
+
+    pl.semaphore_wait(barrier, len(greeted))
     halo = [
         pltpu.make_async_remote_copy(
             src_ref=hs.at[k], dst_ref=hr.at[1 - k], send_sem=hs_sem.at[k], recv_sem=hr_sem.at[1 - k],
@@ -113,6 +113,16 @@
         )
         for k in range(2)
     ]
+    for copy in halo:
+        copy.start()
+    for k in range(2):
+        pl.semaphore_signal(word_sem.at[k], inc=1, device_id=seg(4 * k - 2), device_id_type=MESH)
+
+    cv[...] = conductivity(mv[...])
+    for h in range(2):
+        trans[h] = cv[128 * h : 128 * h + 128, :].T
+        xs[0, h : h + 1, :] = trans[h, 0:1, :]
+        xs[1, h : h + 1, :] = trans[h, 127:128, :]
     halo_x = [
         pltpu.make_async_remote_copy(
             src_ref=xs.at[k], dst_ref=xr.at[1 - k], send_sem=xs_sem.at[k], recv_sem=xr_sem.at[1 - k],
@@ -120,7 +130,7 @@
         )
         for k in range(2)
     ]
-    for copy in halo + halo_x:
+    for copy in halo_x:
         copy.start()
 
     shape = (2, 8, 128)
@@ -219,7 +229,6 @@
 
     for copy in halo:
         copy.wait_recv()
-    low, high = pl.ds(0, 8, stride=32), pl.ds(31, 8, stride=32)
     flux = face(hs[1, 1], hr[1, 1]) * (hr[1, 0] - hs[1, 0])
     fv[high, :] = fv[high, :] + jnp.where(gy < NGY - 1, flux, 0.0)
     flux = face(hs[0, 1], hr[0, 1]) * (hs[0, 0] - hr[0, 0])
@@ -246,6 +255,8 @@
     whole = (pa * og, oal + pa * obe, pb * obe, os1 + pa * os2, pb * os2)
     for k in range(5):
         mine[k] = whole[k]
+    for k in range(2):
+        pl.semaphore_wait(word_sem.at[k], 1)
     near_copies = [
         pltpu.make_async_remote_copy(
             src_ref=mine, dst_ref=near.at[k], send_sem=ns_sem.at[k], recv_sem=nr_sem.at[k],
@@ -333,7 +344,7 @@
     dma = pltpu.SemaphoreType.DMA
     out = pl.pallas_call(
         kernel,
-        out_shape=jax.ShapeDtypeStruct(flat, f32),
+        out_shape=pltpu.VMEM(flat, f32),
         in_specs=[hbm, hbm, hbm, pl.BlockSpec(memory_space=pltpu.SMEM)],
         out_specs=pl.BlockSpec(memory_space=pltpu.VMEM),
         scratch_shapes=[
@@ -344,7 +355,6 @@
             pltpu.VMEM(flat, f32),
             pltpu.VMEM((2, 128, 128), f32),
             pltpu.VMEM((3, 16, 2, 8, 128), f32),
-            pltpu.VMEM((8, 128), f32),
             pltpu.VMEM((14, 2, 8, 128), f32),
             pltpu.VMEM((2, 2, 8, 128), f32),
             pltpu.VMEM((2, 2, 8, 128), f32),
@@ -364,6 +374,7 @@
             dma((len(NEAR),)),
             dma((len(FAR),)),
             dma((len(FAR),)),
+            pltpu.SemaphoreType.REGULAR((2,)),
         ],
         compiler_params=pltpu.CompilerParams(collective_id=0, has_side_effects=True),
         name="adi_x",

time: 33.9 us -> 29.7 us (0.88)
  Pallas kernels: 32.1 us -> 28.7 us
  local copies, waits for them, and re-layouts: 1.57 us -> 0.66 us
    pallas_call x1, Pallas kernels: 32.1 us -> 28.7 us  [local(): pl.pallas_call(kernel, out_shape=pltpu.VMEM(flat, f32), in_specs=[hbm, hb...]
    unnamed x1, local copies, waits for them, and re-layouts: 1.57 us -> 0.66 us
where the time goes in v2:
time: 29.7 us; the launch traced here: 29.4 us
  Pallas kernels  28.7 us (97%)
  local copies, waits for them, and re-layouts  0.66 us (2%)
    pallas_call x1, Pallas kernels, local(): pl.pallas_call(kernel, out_shape=pltpu.VMEM(flat, f32), in_specs=[hbm, hb...  28.7 us
    unnamed x1, local copies, waits for them, and re-layouts  0.66 us

profile of v2, /device:TPU:6, one launch (start us, length us, event | category | flops | bytes accessed | tf_op | source)
XLA Modules:
  0.0 29.4 jit_solution(9427801339629142598)
XLA Ops:
  0.0 28.7 %adi_x.1 = f32[256,128]{1,0:T(8,128)S(1)} custom-call(f32[256,128]{1,0:T(8,128)} %bitcast.5, s32[256,128]{1,0:T(8,128)} %bitcast.6, s32[256,128]{1,0:T(8,128)} %bitcast.7, f32[3]{0:T(128)} %table.1), custom_call_target="tpu_custom_call" | custom-call | tf_op jit(solution)/shard_map/adi_x/pallas_call | solution.py:345
  28.7 0.7 %copy.6 = f32[8,32,128]{2,1,0:T(8,128)} copy(f32[8,32,128]{2,1,0:T(8,128)S(1)} %bitcast.4) | data formatting | bytes 262144

commit v3 on v2

--- a/solution.py
+++ b/solution.py
@@ -68,18 +68,11 @@
 
 
 def kernel(
-    t_hbm, m_hbm, b_hbm, table, out_ref,
-    tv, mv, bv, cv, fv, trans, pq, elim, hs, hr, xs, xr, own, mine, near, mid, far,
+    t_hbm, m_hbm, b_hbm, table_hbm, out_ref,
+    table, tv, mv, bv, cv, fv, trans, pq, elim, hs, hr, xs, xr, own, mine, near, mid, far,
     load_sem, hs_sem, hr_sem, xs_sem, xr_sem, ns_sem, nr_sem, fs_sem, fr_sem, word_sem,
 ):
     gx, gy = lax.axis_index("gx"), lax.axis_index("gy")
-
-    loads = [
-        pltpu.make_async_copy(src, dst, load_sem.at[k])
-        for k, (src, dst) in enumerate(((m_hbm, mv), (t_hbm, tv), (b_hbm, bv)))
-    ]
-    for load in loads:
-        load.start()
 
     def seg(offset):
         return {"gx": lax.rem(gx + (offset % NSEG), NSEG)}
@@ -92,20 +85,30 @@
     for device in greeted:
         pl.semaphore_signal(barrier, inc=1, device_id=device, device_id_type=MESH)
 
+    loads = [
+        pltpu.make_async_copy(src, dst, load_sem.at[k])
+        for k, (src, dst) in enumerate(((table_hbm, table), (m_hbm, mv), (t_hbm, tv), (b_hbm, bv)))
+    ]
+    for load in loads:
+        load.start()
+    pl.semaphore_wait(barrier, len(greeted))
+    for k in range(2):
+        pl.semaphore_signal(word_sem.at[k], inc=1, device_id=seg(4 * k - 2), device_id_type=MESH)
+
+    loads[0].wait()
     t0, t1, t2 = table[0], table[1], table[2]
 
     def conductivity(m):
         return jnp.where(m == 0, t0, jnp.where(m == 1, t1, t2))
 
     low, high = pl.ds(0, 8, stride=32), pl.ds(31, 8, stride=32)
-    loads[0].wait()
+    loads[1].wait()
     hs[0, 1] = conductivity(mv[low, :])
     hs[1, 1] = conductivity(mv[high, :])
-    loads[1].wait()
+    loads[2].wait()
     hs[0, 0] = tv[low, :]
     hs[1, 0] = tv[high, :]
 
-    pl.semaphore_wait(barrier, len(greeted))
     halo = [
         pltpu.make_async_remote_copy(
             src_ref=hs.at[k], dst_ref=hr.at[1 - k], send_sem=hs_sem.at[k], recv_sem=hr_sem.at[1 - k],
@@ -115,8 +118,6 @@
     ]
     for copy in halo:
         copy.start()
-    for k in range(2):
-        pl.semaphore_signal(word_sem.at[k], inc=1, device_id=seg(4 * k - 2), device_id_type=MESH)
 
     cv[...] = conductivity(mv[...])
     for h in range(2):
@@ -211,7 +212,7 @@
     for k, (_, _, _, _, _, r) in enumerate(steps):
         elim[k] = r
 
-    loads[2].wait()
+    loads[3].wait()
     line = lax.broadcasted_iota(jnp.int32, (32, 128), 0)
     below = None
     for z in range(8):
@@ -255,8 +256,6 @@
     whole = (pa * og, oal + pa * obe, pb * obe, os1 + pa * os2, pb * os2)
     for k in range(5):
         mine[k] = whole[k]
-    for k in range(2):
-        pl.semaphore_wait(word_sem.at[k], 1)
     near_copies = [
         pltpu.make_async_remote_copy(
             src_ref=mine, dst_ref=near.at[k], send_sem=ns_sem.at[k], recv_sem=nr_sem.at[k],
@@ -264,7 +263,11 @@
         )
         for k, o in enumerate(NEAR)
     ]
-    for k in (6, 5, 0, 4, 1, 3, 2):
+    for k in (4, 2, 3):
+        near_copies[k].start()
+    for k in range(2):
+        pl.semaphore_wait(word_sem.at[k], 1)
+    for k in (6, 0, 5, 1):
         near_copies[k].start()
 
     steps = [(node, lo, hi, pa, pb, elim[k]) for k, (node, lo, hi, pa, pb, _) in enumerate(steps)]
@@ -345,9 +348,10 @@
     out = pl.pallas_call(
         kernel,
         out_shape=pltpu.VMEM(flat, f32),
-        in_specs=[hbm, hbm, hbm, pl.BlockSpec(memory_space=pltpu.SMEM)],
+        in_specs=[hbm] * 4,
         out_specs=pl.BlockSpec(memory_space=pltpu.VMEM),
         scratch_shapes=[
+            pltpu.SMEM((3,), f32),
             pltpu.VMEM(flat, f32),
             pltpu.VMEM(flat, jnp.int32),
             pltpu.VMEM(flat, jnp.int32),
@@ -365,7 +369,7 @@
             pltpu.VMEM((len(NEAR), 5, 2, 128), f32),
             pltpu.VMEM((3, 5, 2, 128), f32),
             pltpu.VMEM((len(FAR), 5, 2, 128), f32),
-            dma((3,)),
+            dma((4,)),
             dma((2,)),
             dma((2,)),
             dma((2,)),

time: 29.7 us -> 29.2 us (0.983)
  Pallas kernels: 28.7 us -> 28.2 us
    pallas_call x1, Pallas kernels: 28.7 us -> 28.2 us  [local(): pl.pallas_call(kernel, out_shape=pltpu.VMEM(flat, f32), in_specs=[hbm] *...]
where the time goes in v3:
time: 29.2 us; the launch traced here: 28.9 us
  Pallas kernels  28.2 us (97%)
  local copies, waits for them, and re-layouts  0.66 us (2%)
    pallas_call x1, Pallas kernels, local(): pl.pallas_call(kernel, out_shape=pltpu.VMEM(flat, f32), in_specs=[hbm] *...  28.2 us
    unnamed x1, local copies, waits for them, and re-layouts  0.66 us

profile of v3, /device:TPU:6, one launch (start us, length us, event | category | flops | bytes accessed | tf_op | source)
XLA Modules:
  0.0 28.9 jit_solution(10646089566631152999)
XLA Ops:
  0.0 28.2 %adi_x.1 = f32[256,128]{1,0:T(8,128)S(1)} custom-call(f32[256,128]{1,0:T(8,128)} %bitcast.5, s32[256,128]{1,0:T(8,128)} %bitcast.6, s32[256,128]{1,0:T(8,128)} %bitcast.7, f32[3]{0:T(128)} %table_hbm.1), custom_call_target="tpu_custom_call" | custom-call | tf_op jit(solution)/shard_map/adi_x/pallas_call | solution.py:348
  28.2 0.7 %copy.6 = f32[8,32,128]{2,1,0:T(8,128)} copy(f32[8,32,128]{2,1,0:T(8,128)S(1)} %bitcast.4) | data formatting | bytes 262144

commit v4 on v3

--- a/solution.py
+++ b/solution.py
@@ -9,7 +9,7 @@
 RATIO = 65536.0
 NSEG = 64
 NGY = 8
-NEAR = (-3, -2, -1, 1, 2, 3, 4)
+NEAR = (-4, -3, -2, -1, 1, 2, 3)
 GREET = (-2, -1, 1, 2, 16, 32, 48)
 FAR = (4, 12, 20, 28, 36, 44, 52, 60)
 
@@ -91,10 +91,6 @@
     ]
     for load in loads:
         load.start()
-    pl.semaphore_wait(barrier, len(greeted))
-    for k in range(2):
-        pl.semaphore_signal(word_sem.at[k], inc=1, device_id=seg(4 * k - 2), device_id_type=MESH)
-
     loads[0].wait()
     t0, t1, t2 = table[0], table[1], table[2]
 
@@ -109,6 +105,15 @@
     hs[0, 0] = tv[low, :]
     hs[1, 0] = tv[high, :]
 
+    cv[...] = conductivity(mv[...])
+    for h in range(2):
+        trans[h] = cv[128 * h : 128 * h + 128, :].T
+        xs[0, h : h + 1, :] = trans[h, 0:1, :]
+        xs[1, h : h + 1, :] = trans[h, 127:128, :]
+    pl.semaphore_wait(barrier, len(greeted))
+    for k in range(2):
+        pl.semaphore_signal(word_sem.at[k], inc=1, device_id=seg(4 * k - 2), device_id_type=MESH)
+
     halo = [
         pltpu.make_async_remote_copy(
             src_ref=hs.at[k], dst_ref=hr.at[1 - k], send_sem=hs_sem.at[k], recv_sem=hr_sem.at[1 - k],
@@ -119,11 +124,6 @@
     for copy in halo:
         copy.start()
 
-    cv[...] = conductivity(mv[...])
-    for h in range(2):
-        trans[h] = cv[128 * h : 128 * h + 128, :].T
-        xs[0, h : h + 1, :] = trans[h, 0:1, :]
-        xs[1, h : h + 1, :] = trans[h, 127:128, :]
     halo_x = [
         pltpu.make_async_remote_copy(
             src_ref=xs.at[k], dst_ref=xr.at[1 - k], send_sem=xs_sem.at[k], recv_sem=xr_sem.at[1 - k],
@@ -263,11 +263,11 @@
         )
         for k, o in enumerate(NEAR)
     ]
-    for k in (4, 2, 3):
+    for k in (2, 3, 4):
         near_copies[k].start()
     for k in range(2):
         pl.semaphore_wait(word_sem.at[k], 1)
-    for k in (6, 0, 5, 1):
+    for k in (0, 1, 6, 5):
         near_copies[k].start()
 
     steps = [(node, lo, hi, pa, pb, elim[k]) for k, (node, lo, hi, pa, pb, _) in enumerate(steps)]
@@ -296,15 +296,15 @@
         copy.wait_recv()
     item = {o: tuple(near[k, i] for i in range(5)) for k, o in enumerate(NEAR)}
     item[0] = whole
-    ahead = combine(combine(item[1], item[2]), combine(item[3], item[4]))
-    behind = combine(item[-3], item[-2])
-    behind_own = combine(behind, combine(item[-1], item[0]))
-    behind = combine(behind, item[-1])
-    window = combine(behind_own, ahead)
+    behind = combine(combine(item[-4], item[-3]), combine(item[-2], item[-1]))
+    ahead = combine(item[2], item[3])
+    own_ahead = combine(combine(item[0], item[1]), ahead)
+    ahead = combine(item[1], ahead)
+    window = combine(behind, own_ahead)
     for k in range(5):
-        mid[0, k] = ahead[k]
+        mid[0, k] = own_ahead[k]
         mid[1, k] = window[k]
-        mid[2, k] = behind_own[k]
+        mid[2, k] = behind[k]
     far_copies = [
         pltpu.make_async_remote_copy(
             src_ref=mid.at[0 if k == 0 else 2 if k == 7 else 1], dst_ref=far.at[k],

time: 29.2 us -> 28.4 us (0.973)
  Pallas kernels: 28.2 us -> 27.4 us
    pallas_call x1, Pallas kernels: 28.2 us -> 27.4 us  [local(): pl.pallas_call(kernel, out_shape=pltpu.VMEM(flat, f32), in_specs=[hbm] *...]
where the time goes in v4:
time: 28.4 us; the launch traced here: 28.1 us
  Pallas kernels  27.4 us (96%)
  local copies, waits for them, and re-layouts  0.66 us (2%)
    pallas_call x1, Pallas kernels, local(): pl.pallas_call(kernel, out_shape=pltpu.VMEM(flat, f32), in_specs=[hbm] *...  27.4 us
    unnamed x1, local copies, waits for them, and re-layouts  0.66 us

profile of v4, /device:TPU:6, one launch (start us, length us, event | category | flops | bytes accessed | tf_op | source)
XLA Modules:
  0.0 28.1 jit_solution(16945516107109467944)
XLA Ops:
  0.0 27.4 %adi_x.1 = f32[256,128]{1,0:T(8,128)S(1)} custom-call(f32[256,128]{1,0:T(8,128)} %bitcast.5, s32[256,128]{1,0:T(8,128)} %bitcast.6, s32[256,128]{1,0:T(8,128)} %bitcast.7, f32[3]{0:T(128)} %table_hbm.1), custom_call_target="tpu_custom_call" | custom-call | tf_op jit(solution)/shard_map/adi_x/pallas_call | solution.py:348
  27.4 0.7 %copy.6 = f32[8,32,128]{2,1,0:T(8,128)} copy(f32[8,32,128]{2,1,0:T(8,128)S(1)} %bitcast.4) | data formatting | bytes 262144

commit v5 on v4

--- a/solution.py
+++ b/solution.py
@@ -10,7 +10,7 @@
 NSEG = 64
 NGY = 8
 NEAR = (-4, -3, -2, -1, 1, 2, 3)
-GREET = (-2, -1, 1, 2, 16, 32, 48)
+GREET = (-3, -2, -1, 1, 2, 16, 32, 48)
 FAR = (4, 12, 20, 28, 36, 44, 52, 60)
 
 
@@ -70,7 +70,7 @@
 def kernel(
     t_hbm, m_hbm, b_hbm, table_hbm, out_ref,
     table, tv, mv, bv, cv, fv, trans, pq, elim, hs, hr, xs, xr, own, mine, near, mid, far,
-    load_sem, hs_sem, hr_sem, xs_sem, xr_sem, ns_sem, nr_sem, fs_sem, fr_sem, word_sem,
+    load_sem, hs_sem, hr_sem, xs_sem, xr_sem, ns_sem, nr_sem, fs_sem, fr_sem,
 ):
     gx, gy = lax.axis_index("gx"), lax.axis_index("gy")
 
@@ -105,15 +105,7 @@
     hs[0, 0] = tv[low, :]
     hs[1, 0] = tv[high, :]
 
-    cv[...] = conductivity(mv[...])
-    for h in range(2):
-        trans[h] = cv[128 * h : 128 * h + 128, :].T
-        xs[0, h : h + 1, :] = trans[h, 0:1, :]
-        xs[1, h : h + 1, :] = trans[h, 127:128, :]
     pl.semaphore_wait(barrier, len(greeted))
-    for k in range(2):
-        pl.semaphore_signal(word_sem.at[k], inc=1, device_id=seg(4 * k - 2), device_id_type=MESH)
-
     halo = [
         pltpu.make_async_remote_copy(
             src_ref=hs.at[k], dst_ref=hr.at[1 - k], send_sem=hs_sem.at[k], recv_sem=hr_sem.at[1 - k],
@@ -123,6 +115,11 @@
     ]
     for copy in halo:
         copy.start()
+    cv[...] = conductivity(mv[...])
+    for h in range(2):
+        trans[h] = cv[128 * h : 128 * h + 128, :].T
+        xs[0, h : h + 1, :] = trans[h, 0:1, :]
+        xs[1, h : h + 1, :] = trans[h, 127:128, :]
 
     halo_x = [
         pltpu.make_async_remote_copy(
@@ -263,11 +260,7 @@
         )
         for k, o in enumerate(NEAR)
     ]
-    for k in (2, 3, 4):
-        near_copies[k].start()
-    for k in range(2):
-        pl.semaphore_wait(word_sem.at[k], 1)
-    for k in (0, 1, 6, 5):
+    for k in (0, 1, 6, 2, 5, 3, 4):
         near_copies[k].start()
 
     steps = [(node, lo, hi, pa, pb, elim[k]) for k, (node, lo, hi, pa, pb, _) in enumerate(steps)]
@@ -378,7 +371,6 @@
             dma((len(NEAR),)),
             dma((len(FAR),)),
             dma((len(FAR),)),
-            pltpu.SemaphoreType.REGULAR((2,)),
         ],
         compiler_params=pltpu.CompilerParams(collective_id=0, has_side_effects=True),
         name="adi_x",

time: 28.4 us -> 28.3 us (level)
  no operation moved by 1% of the time
where the time goes in v5:
time: 28.3 us; the launch traced here: 28.2 us
  Pallas kernels  27.5 us (97%)
  local copies, waits for them, and re-layouts  0.66 us (2%)
    pallas_call x1, Pallas kernels, local(): pl.pallas_call(kernel, out_shape=pltpu.VMEM(flat, f32), in_specs=[hbm] *...  27.5 us
    unnamed x1, local copies, waits for them, and re-layouts  0.66 us

profile of v5, /device:TPU:6, one launch (start us, length us, event | category | flops | bytes accessed | tf_op | source)
XLA Modules:
  0.0 28.2 jit_solution(15444535888376262144)
XLA Ops:
  0.0 27.5 %adi_x.1 = f32[256,128]{1,0:T(8,128)S(1)} custom-call(f32[256,128]{1,0:T(8,128)} %bitcast.5, s32[256,128]{1,0:T(8,128)} %bitcast.6, s32[256,128]{1,0:T(8,128)} %bitcast.7, f32[3]{0:T(128)} %table_hbm.1), custom_call_target="tpu_custom_call" | custom-call | tf_op jit(solution)/shard_map/adi_x/pallas_call | solution.py:341
  27.5 0.7 %copy.6 = f32[8,32,128]{2,1,0:T(8,128)} copy(f32[8,32,128]{2,1,0:T(8,128)S(1)} %bitcast.4) | data formatting | bytes 262144

commit v6 on v5

--- a/solution.py
+++ b/solution.py
@@ -81,9 +81,17 @@
         return {"gy": lax.rem(gy + (offset % NGY), NGY)}
 
     barrier = pltpu.get_barrier_semaphore()
-    greeted = [side(1), side(-1)] + [seg(o) for o in GREET]
+    greeted = [seg(o) for o in GREET]
+    has = (gy > 0, gy < NGY - 1)
+    for k in range(2):
+
+        @pl.when(has[k])
+        def _():
+            pl.semaphore_signal(barrier, inc=1, device_id=side(2 * k - 1), device_id_type=MESH)
+
     for device in greeted:
         pl.semaphore_signal(barrier, inc=1, device_id=device, device_id_type=MESH)
+    met = len(greeted) + jnp.where(has[0], 1, 0) + jnp.where(has[1], 1, 0)
 
     loads = [
         pltpu.make_async_copy(src, dst, load_sem.at[k])
@@ -105,7 +113,7 @@
     hs[0, 0] = tv[low, :]
     hs[1, 0] = tv[high, :]
 
-    pl.semaphore_wait(barrier, len(greeted))
+    pl.semaphore_wait(barrier, met)
     halo = [
         pltpu.make_async_remote_copy(
             src_ref=hs.at[k], dst_ref=hr.at[1 - k], send_sem=hs_sem.at[k], recv_sem=hr_sem.at[1 - k],
@@ -113,8 +121,8 @@
         )
         for k in range(2)
     ]
-    for copy in halo:
-        copy.start()
+    for k in range(2):
+        pl.when(has[k])(halo[k].start)
     cv[...] = conductivity(mv[...])
     for h in range(2):
         trans[h] = cv[128 * h : 128 * h + 128, :].T
@@ -225,8 +233,8 @@
             value = value + below
         fv[here, :] = value
 
-    for copy in halo:
-        copy.wait_recv()
+    for k in range(2):
+        pl.when(has[1 - k])(halo[k].wait_recv)
     flux = face(hs[1, 1], hr[1, 1]) * (hr[1, 0] - hs[1, 0])
     fv[high, :] = fv[high, :] + jnp.where(gy < NGY - 1, flux, 0.0)
     flux = face(hs[0, 1], hr[0, 1]) * (hs[0, 0] - hr[0, 0])
@@ -329,7 +337,9 @@
     for h in range(2):
         out_ref[128 * h : 128 * h + 128, :] = trans[h].T
 
-    for copy in halo + halo_x + near_copies + far_copies:
+    for k in range(2):
+        pl.when(has[k])(halo[k].wait_send)
+    for copy in halo_x + near_copies + far_copies:
         copy.wait_send()
 
 

time: 28.3 us -> 28.4 us (level)
  no operation moved by 1% of the time
where the time goes in v6:
time: 28.4 us; the launch traced here: 28.3 us
  Pallas kernels  27.6 us (97%)
  local copies, waits for them, and re-layouts  0.66 us (2%)
    pallas_call x1, Pallas kernels, local(): pl.pallas_call(kernel, out_shape=pltpu.VMEM(flat, f32), in_specs=[hbm] *...  27.6 us
    unnamed x1, local copies, waits for them, and re-layouts  0.66 us

profile of v6, /device:TPU:6, one launch (start us, length us, event | category | flops | bytes accessed | tf_op | source)
XLA Modules:
  0.0 28.3 jit_solution(9678495425390499663)
XLA Ops:
  0.0 27.6 %adi_x.1 = f32[256,128]{1,0:T(8,128)S(1)} custom-call(f32[256,128]{1,0:T(8,128)} %bitcast.5, s32[256,128]{1,0:T(8,128)} %bitcast.6, s32[256,128]{1,0:T(8,128)} %bitcast.7, f32[3]{0:T(128)} %table_hbm.1), custom_call_target="tpu_custom_call" | custom-call | tf_op jit(solution)/shard_map/adi_x/pallas_call | solution.py:351
  27.6 0.7 %copy.6 = f32[8,32,128]{2,1,0:T(8,128)} copy(f32[8,32,128]{2,1,0:T(8,128)S(1)} %bitcast.4) | data formatting | bytes 262144

commit v7 on v4

--- a/solution.py
+++ b/solution.py
@@ -315,12 +315,14 @@
     ]
     for k in (3, 4, 2, 5, 1, 6, 0, 7):
         far_copies[k].start()
-    for copy in far_copies:
-        copy.wait_recv()
-    chain = [ahead] + [tuple(far[k, i] for i in range(5)) for k in range(8)] + [behind]
-    while len(chain) > 1:
-        chain = [combine(*chain[k : k + 2]) if k + 1 < len(chain) else chain[k] for k in range(0, len(chain), 2)]
-    _, right_g, left_g, right_s, left_s = chain[0]
+    def arrived(k):
+        far_copies[k].wait_recv()
+        return tuple(far[k, i] for i in range(5))
+
+    head = combine(combine(ahead, arrived(0)), combine(arrived(1), arrived(2)))
+    tail = combine(arrived(6), combine(arrived(7), behind))
+    centre = combine(combine(arrived(3), arrived(4)), arrived(5))
+    _, right_g, left_g, right_s, left_s = combine(combine(head, centre), tail)
 
     r = og / (og + right_g)
     end_g, end_s = obe + r * right_g, os2 + r * right_s

time: 28.4 us -> 28.4 us (level)
  no operation moved by 1% of the time
where the time goes in v7:
time: 28.4 us; the launch traced here: 28.1 us
  Pallas kernels  27.5 us (97%)
  local copies, waits for them, and re-layouts  0.66 us (2%)
    pallas_call x1, Pallas kernels, local(): pl.pallas_call(kernel, out_shape=pltpu.VMEM(flat, f32), in_specs=[hbm] *...  27.5 us
    unnamed x1, local copies, waits for them, and re-layouts  0.66 us

profile of v7, /device:TPU:6, one launch (start us, length us, event | category | flops | bytes accessed | tf_op | source)
XLA Modules:
  0.0 28.1 jit_solution(3309750356104273632)
XLA Ops:
  0.0 27.5 %adi_x.1 = f32[256,128]{1,0:T(8,128)S(1)} custom-call(f32[256,128]{1,0:T(8,128)} %bitcast.5, s32[256,128]{1,0:T(8,128)} %bitcast.6, s32[256,128]{1,0:T(8,128)} %bitcast.7, f32[3]{0:T(128)} %table_hbm.1), custom_call_target="tpu_custom_call" | custom-call | tf_op jit(solution)/shard_map/adi_x/pallas_call | solution.py:350
  27.5 0.7 %copy.6 = f32[8,32,128]{2,1,0:T(8,128)} copy(f32[8,32,128]{2,1,0:T(8,128)S(1)} %bitcast.4) | data formatting | bytes 262144
